TPU v7x, 256 devices: a whole 4x4x8 slice. The times are simulated.
256 devices in a mesh: tm: 32 (over y, x, core), space: 8 (over z).
Axes of the slice: x: 4, y: 4, z: 8, core: 2. Of those that a mesh axis runs over, the one named last changes fastest.
Arguments:
- latent_tokens: bfloat16 [64, 1792, 2240], P('tm', 'space'), may hold values from -6 to 6
- norm_gain: float32 [2240], replicated, may hold values from 0.5 to 1.5
- w_query: bfloat16 [2240, 1120], P('tm', 'space'), may hold values from -0.125 to 0.125
- w_key: bfloat16 [2240, 1120], P('tm', 'space'), may hold values from -0.125 to 0.125
- w_value: bfloat16 [2240, 1120], P('tm', 'space'), may hold values from -0.125 to 0.125
- out_gain: float32 [1120], replicated, may hold values from 0.5 to 1.5
- block_ids: int32 [64], P('tm'), may hold values from 0 to 15, never falling along the last dimension, each value on 1 to 8 neighbouring positions
Outputs:
- attended: bfloat16 [64, 1792, 1120], P('tm', 'space')
Inputs may be any that keep to these rules, and one draw needn't show every extreme that they name: `block_ids`: block numbers never fall from one frame to the next; each of the 16 blocks holds 1 to 8 frames and one holds exactly 8.
All inputs are finite; a program needn't handle non-finite values.
Results may differ from a plain program's by a relative error of at most 0.0065.
Values may be sent and summed in bfloat16 or wider, within the bound.
A program may use at most 192 MiB of HBM per device.

v0:
```python
import jax
import jax.numpy as jnp
from jax import lax
from jax.sharding import PartitionSpec as P

HEAD = 112
HEADS = 10


def prefix(value, axis, join, neutral):
    count, mine = (lax.axis_size(axis), lax.axis_index(axis))
    pieces = lax.all_gather(value, axis)
    so_far = jnp.full_like(value, 0) + jnp.asarray(neutral, value.dtype)

    def step(position, so_far):
        longer = join(so_far, pieces[position])
        return jnp.where(position < mine, longer, so_far)

    return lax.fori_loop(0, count - 1, step, so_far)


def carried_in(x, axis, join, neutral):
    count = lax.axis_size(axis)
    place = lax.axis_index(axis)
    ahead = count - 1 - place
    gathered = jax.tree.map(
        lambda a, kind: lax.all_gather(a.astype(kind), axis),
        x,
        jax.tree.map(lambda a: jnp.bfloat16 if a.dtype == jnp.float32 else a.dtype, x),
    )
    state = jax.tree.map(lambda a, e: jnp.zeros_like(a) + jnp.asarray(e, a.dtype), x, neutral)

    def one(step, state):
        source = count - 1 - step
        return join(
            state,
            jax.tree.map(
                lambda a, own: lax.dynamic_index_in_dim(a, source, 0, False).astype(own.dtype),
                gathered,
                x,
            ),
        )

    return lax.fori_loop(0, ahead, one, state)


def add_states(earlier, later):
    return earlier + later


def join_later(earlier, later):
    high_vacant, high_leading, high_uniform, high_running = earlier
    low_vacant, low_leading, low_uniform, low_running = later
    matching = (high_leading == low_leading).astype(jnp.float32)
    joined = low_uniform * matching * (1.0 - high_vacant)
    low_absent = low_vacant > 0.5
    leading = jnp.where(low_absent, high_leading, low_leading)
    vacant = low_vacant * high_vacant
    uniform = jnp.where(
        low_absent,
        high_uniform,
        low_uniform * (high_vacant + (1.0 - high_vacant) * high_uniform * matching),
    )
    running = jnp.where(low_absent, high_running, low_running + joined * high_running)
    return (vacant, leading, uniform, running)


def on_device(latent_tokens, norm_gain, w_query, w_key, w_value, out_gain, block_ids):
    frame_count, token_count, width = latent_tokens.shape
    row_count = frame_count * token_count
    values = latent_tokens.reshape(row_count, width).astype(jnp.float32)
    meansq = jnp.mean(values * values, axis=-1, keepdims=True)
    normed = (values * lax.rsqrt(meansq + 1e-06) * norm_gain).astype(jnp.bfloat16)
    stacked = jnp.stack((w_query, w_key, w_value))
    columns_full = lax.all_gather(stacked, "space", axis=2, tiled=True)
    projected = jnp.einsum(
        "rn,cnh->crh",
        normed,
        lax.all_gather(columns_full, "tm", axis=1, tiled=True),
        preferred_element_type=jnp.float32,
    )
    channels = projected.shape[2]
    query = jax.nn.relu(projected[0]).reshape(frame_count, token_count, HEADS, HEAD)
    key = (
        jax.nn.relu(projected[1])
        .astype(jnp.bfloat16)
        .reshape(frame_count, token_count, HEADS, HEAD)
    )
    value = projected[2].astype(jnp.bfloat16).reshape(frame_count, token_count, HEADS, HEAD)
    local_states = jnp.einsum("fthk,fthv->fhkv", key, value, preferred_element_type=jnp.float32)
    per_frame_state = lax.psum(local_states, "space")
    device_sum = jnp.sum(per_frame_state, axis=0)
    zero_state = jnp.zeros_like(device_sum)
    before = prefix(device_sum, "tm", add_states, zero_state)
    leading_id = block_ids[0]
    closing_id = block_ids[frame_count - 1]
    within_leading = (block_ids == leading_id).astype(jnp.float32)
    leading_sum = jnp.einsum(
        "o,owpe->wpe", within_leading, per_frame_state, precision=lax.Precision.HIGHEST
    )
    uniform_flag = jnp.min(within_leading)
    leading_float = leading_id.astype(jnp.float32)
    closing_float = closing_id.astype(jnp.float32)
    summary = (jnp.float32(0.0), leading_float, uniform_flag, leading_sum)
    identity = (jnp.float32(1.0), jnp.float32(0.0), jnp.float32(1.0), zero_state)
    vacant, leading, uniform, running = carried_in(summary, "tm", join_later, identity)
    reaches = (1.0 - vacant) * (leading == closing_float).astype(jnp.float32)
    trailing = reaches * running
    earlier_mask = (block_ids[None, :] <= block_ids[:, None]).astype(jnp.float32)
    in_closing = (block_ids == closing_id).astype(jnp.float32)
    carried = before[None] + jnp.einsum(
        "ij,jhkv->ihkv", earlier_mask, per_frame_state, precision=lax.Precision.HIGHEST
    )
    carried = carried + in_closing[:, None, None, None] * trailing[None]
    numerator = jnp.einsum("fthk,fhkv->fthv", query, carried, precision=lax.Precision.HIGHEST)
    head_meansq = jnp.mean(numerator * numerator, axis=-1, keepdims=True)
    result = numerator * lax.rsqrt(head_meansq + 1e-06) * out_gain.reshape(HEADS, HEAD)
    return result.reshape(frame_count, token_count, channels).astype(jnp.bfloat16)


def solution(mesh):
    placed = (
        P("tm", "space", None),
        P(),
        P("tm", "space"),
        P("tm", "space"),
        P("tm", "space"),
        P(),
        P("tm"),
    )
    return jax.shard_map(
        on_device, mesh=mesh, in_specs=placed, out_specs=P("tm", "space", None), check_vma=False
    )
```

profile of v0, /device:TPU:32, one launch (start us, length us, event | category | flops | bytes accessed | tf_op | source)
XLA Modules:
  0.0 544.3 jit_solution(14924308415363143273)
XLA Ops:
  7.7 29.9 %all_gather.33 = bf16[3,70,1120]{1,0,2:T(4,128)(2,1)S(1)} all-gather(bf16[3,70,140]{1,0,2:T(4,128)(2,1)S(1)} %copy.37), channel_id=1, replica_groups=mesh['tm'=32,'space'=8] {'space'}, dimensions={2}, use_global_device_ids=true | all-gather | bytes 529200 | tf_op jit(solution)/shard_map/all_gather | solution.py:75
  37.6 2.2 copy.38
  40.5 1.9 fusion.7
  42.4 84.1 %all-gather.6.cloned.1.call-done = bf16[3,2240,1120]{2,0,1:T(4,128)(2,1)} async-done(((bf16[3,70,1120]{2,0,1:T(4,128)(2,1)}), bf16[3,2240,1120]{2,0,1:T(4,128)(2,1)}) %all-gather.6.cloned.1.call-update) | async-done | bytes 15052816 | tf_op jit(solution)/shard_map/all_gather | solution.py:79
  126.5 14.1 %fusion.3 = f32[3,448,1120]{2,1,0:T(8,128)S(1)} fusion(bf16[3,2240,1120]{2,0,1:T(4,128)(2,1)} %all-gather.6.cloned.1.call-done, bf16[448,2240]{1,0:T(8,128)(2,1)} %fusion.7), kind=kOutput, calls=%fused_computation.5 | convolution fusion | flops 6743654400 | bytes 23080960 | tf_op jit(solution)/shard_map/rn,cnh->crh/dot_general | solution.py:76
  140.7 1.4 fusion.13
  142.1 1.5 copy-done.2
  143.6 3.4 reshape.84
  147.0 3.1 reshape.83
  150.1 3.1 fusion.16
  153.9 75.4 %all-reduce.6.cloned.1.call-done = f32[2,10,112,112]{3,2,1,0:T(8,128)} async-done(((f32[2,10,112,112]{3,2,1,0:T(8,128)}), f32[2,10,112,112]{3,2,1,0:T(8,128)}) %all-reduce.6.cloned.1.call-update) | async-done | bytes 1003536 | tf_op jit(solution)/shard_map/psum | solution.py:91
  229.3 4.7 fusion.20
  239.7 1.3 dynamic-update-slice.2
  241.0 63.4 %all-reduce.3 = (bf16[32]{0:T(256)(128)(2,1)S(1)}, bf16[32]{0:T(256)(128)(2,1)S(1)}, bf16[32]{0:T(256)(128)(2,1)S(1)}) all-reduce(bf16[32]{0:T(256)(128)(2,1)S(1)} %dynamic-update-slice, bf16[32]{0:T(256)(128)(2,1)S(1)} %dynamic-update-slice.1, bf16[32]{0:T(256)(128)(2,1)S(1)} %dynamic-update-slice.2), channel_id=1, replica_groups=mesh['tm'=32,'space'=8] {'tm'}, use_global_device_ids=true, to_apply=%add | all-reduce | flops 96 | bytes 384
  305.6 1.7 slice_maximum_fusion
  307.4 3.3 reshape.85
  310.7 177.9 %while.32 = (s32[]{:T(128)}, f32[]{:T(128)}, f32[]{:T(128)}, f32[10,112,112]{2,1,0:T(8,128)S(1)}, s32[]{:T(128)}, /*index=5*/bf16[32]{0:T(256)(128)(2,1)S(1)}, b...) while((s32[]{:T(128)}, f32[]{:T(128)}, f32[]{:T(128)}, ...), condition=%wide.region_7.8_spmd, body=%wide.region_6.7_spmd.sunk | while | flops 501773 | bytes 1254722 | solution.py:44
  320.9 1.3 fusion.33
  361.1 1.3 fusion.33
  488.6 38.9 %while.33 = (s32[]{:T(128)}, f32[10,112,112]{2,1,0:T(8,128)S(1)}, s32[]{:T(128)}, f32[32,10,112,112]{3,2,1,0:T(8,128)}, s32[]{:T(128)}, /*index=5*/s32[]{:T(128)}) while((s32[]{:T(128)}, f32[10,112,112]{2,1,0:T(8,128)S(1)}, s32[]{:T(128)}, f32[32,10,112,112]{3,2,1,0:T(8,128)}, s32[]{:T(128)}, /*index=5*/s32[]{:T(128)}) %tuple.73), condition=%wide.region_4.5_spmd.clone, body=%wide.region_3.4_spmd.clone.sunk | while | flops 376324 | bytes 1505381 | solution.py:19
  488.6 1.3 add_select_fusion.2
  527.6 3.3 fusion.15
  530.9 5.1 fusion.8
  536.4 1.4 copy.48
  (201 shorter events, 133.8 us)
Async XLA Ops:
  6.5 120.0 %all-gather.6.cloned.1.call-start = ((), (), s32[]{:S(2)}) async-start(), calls=%async_computation | async-start | bytes 21288960 | tf_op jit(solution)/shard_map/all_gather | solution.py:79
  6.5 33.4 %copy-start.1 = (bf16[2,224,2240]{2,1,0:T(8,128)(2,1)S(1)}, bf16[2,224,2240]{2,1,0:T(8,128)(2,1)}, u32[]{:S(2)}) copy-start(bf16[2,224,2240]{2,1,0:T(8,128)(2,1)} %param.11) | copy-start | bytes 6021124
  37.6 2.9 copy-start.5
  39.9 189.4 %all-reduce.6.cloned.1.call-start = ((), (), s32[]{:S(2)}) async-start(), calls=%async_computation.1 | async-start | bytes 2293760 | tf_op jit(solution)/shard_map/psum | solution.py:91
  140.7 2.9 copy-start.2
  150.1 3.2 copy-start.7
  153.3 157.4 %all-gather.10.cloned.1.call-start = ((), (), s32[]{:S(2)}) async-start(), calls=%async_computation.3 | async-start | bytes 9461760 | tf_op jit(solution)/shard_map/all_gather | solution.py:27
  229.3 5.6 %copy-start.3 = (f32[2,10,112,112]{3,2,1,0:T(8,128)S(1)}, f32[2,10,112,112]{3,2,1,0:T(8,128)}, u32[]{:S(2)}) copy-start(f32[2,10,112,112]{3,2,1,0:T(8,128)} %all-reduce.6.cloned.1.call-done) | copy-start | bytes 3010564
  234.0 2.5 copy-start.8
  234.0 71.0 %copy-start.6 = (f32[1120]{0:T(1024)S(1)}, f32[1120]{0:T(1024)}, u32[]{:S(2)}) copy-start(f32[1120]{0:T(1024)} %param.16) | copy-start | bytes 13444
  234.8 253.8 %all-gather.8.cloned.1.call-start = ((), (), s32[]{:S(2)}) async-start(), calls=%async_computation.2 | async-start | bytes 18923520 | tf_op jit(solution)/shard_map/all_gather | solution.py:12
  488.6 38.9 %copy-start.4 = (f32[2,10,112,112]{3,2,1,0:T(8,128)S(1)}, f32[2,10,112,112]{3,2,1,0:T(8,128)}, u32[]{:S(2)}) copy-start(f32[2,10,112,112]{3,2,1,0:T(8,128)} %all-reduce.6.cloned.1.call-done) | copy-start | bytes 3010564
  527.6 3.3 copy-start
Sparse Core Ops, SparseCore 0:
  40.0 86.5 all-gather.5
  153.4 75.8 all-reduce.5
  235.0 58.7 all-gather.9
  296.1 80.6 all-gather.7
where the time goes:
time: 548 us; the launch traced here: 544 us
  waiting for transfers between devices  160 us (29%)
  blocking collectives  93.3 us (17%)
  loops' own time  87.7 us (16%)
  other arithmetic  87.5 us (16%)
  local copies, waits for them, and re-layouts  71.2 us (13%)
  matrix products  30.4 us (6%)
  between operations  14.5 us (3%)
    another operation x1, loops' own time, carried_in(): return lax.fori_loop(0, ahead, one, state)  86.9 us
    all_gather x1, waiting for transfers between devices, on_device(): lax.all_gather(columns_full, 'tm', axis=1, tiled=True)  84.1 us
    psum x1, waiting for transfers between devices, on_device(): per_frame_state = lax.psum(local_states, 'space')  75.4 us
    unnamed x1, blocking collectives  63.4 us
    dynamic_slice x93, local copies, waits for them, and re-layouts, one(): lax.dynamic_index_in_dim(a, source, 0, False).astype(own.dtype)  52 us
    select_n x31, other arithmetic, join_later(): jnp.where(low_absent, high_running, low_running + joined * high_running)  38.9 us
    select_n x31, other arithmetic, step(): return jnp.where(position < mine, longer, so_far)  38.2 us
    all_gather x1, blocking collectives, on_device(): columns_full = lax.all_gather(stacked, 'space', axis=2, tiled=True)  29.9 us
  transfers between devices with their start and end apart: 4, of which 2 were waited for; matrix products, arithmetic and copies ran while one was open for 19% of the time, Pallas kernels for 0%

commit v1 on v0

--- a/solution.py
+++ b/solution.py
@@ -76,7 +76,9 @@
     projected = jnp.einsum(
         "rn,cnh->crh",
         normed,
-        lax.all_gather(columns_full, "tm", axis=1, tiled=True),
+        jnp.concatenate(
+            lax.all_to_all(jnp.stack([columns_full] * lax.axis_size("tm")), "tm", 0, 0), axis=1
+        ),
         preferred_element_type=jnp.float32,
     )
     channels = projected.shape[2]

time: 548 us -> 713 us (1.30)
  waiting for transfers between devices: 160 us -> 271 us
  local copies, waits for them, and re-layouts: 71.2 us -> 115 us
  starting transfers between devices: 0.13 us -> 7.69 us
    all_to_all x0 -> x1, waiting for transfers between devices: none -> 200 us  [on_device(): lax.all_to_all(jnp.stack([columns_full] * lax.axis_size('tm')), 'tm', 0, 0)]
    all_gather x1 -> x0, waiting for transfers between devices: 84.1 us -> none  [on_device(): lax.all_gather(columns_full, 'tm', axis=1, tiled=True)]
    reshape x0 -> x2, local copies, waits for them, and re-layouts: none -> 34.8 us  [on_device(): jnp.concatenate(lax.all_to_all(jnp.stack([columns_full] * lax.axis_size('...]
    all_to_all x0 -> x1, starting transfers between devices: none -> 7.57 us  [on_device(): lax.all_to_all(jnp.stack([columns_full] * lax.axis_size('tm')), 'tm', 0, 0)]
  transfers between devices with their start and end apart: 4 -> 4, of which waited for: 2 -> 2; matrix products, arithmetic and copies ran while one was open for 19% -> 15% of each run, Pallas kernels for 0% -> 0%
where the time goes in v1:
time: 713 us; the launch traced here: 708 us
  waiting for transfers between devices  271 us (38%)
  local copies, waits for them, and re-layouts  115 us (16%)
  loops' own time  93.6 us (13%)
  blocking collectives  93.3 us (13%)
  other arithmetic  85.8 us (12%)
  matrix products  27.2 us (4%)
  between operations  14.6 us (2%)
  starting transfers between devices  7.69 us (1%)
    all_to_all x1, waiting for transfers between devices, on_device(): lax.all_to_all(jnp.stack([columns_full] * lax.axis_size('tm')), 'tm', 0, 0)  200 us
    another operation x1, loops' own time, carried_in(): return lax.fori_loop(0, ahead, one, state)  92.8 us
    psum x1, waiting for transfers between devices, on_device(): per_frame_state = lax.psum(local_states, 'space')  70.8 us
    unnamed x1, blocking collectives  63.4 us
    dynamic_slice x93, local copies, waits for them, and re-layouts, one(): lax.dynamic_index_in_dim(a, source, 0, False).astype(own.dtype)  53.8 us
    select_n x31, other arithmetic, join_later(): jnp.where(low_absent, high_running, low_running + joined * high_running)  38.9 us
    select_n x31, other arithmetic, step(): return jnp.where(position < mine, longer, so_far)  38.2 us
    reshape x2, local copies, waits for them, and re-layouts, on_device(): jnp.concatenate(lax.all_to_all(jnp.stack([columns_full] * lax.axis_size('...  34.8 us
  transfers between devices with their start and end apart: 4, of which 2 were waited for; matrix products, arithmetic and copies ran while one was open for 15% of the time, Pallas kernels for 0%

profile of v1, /device:TPU:32, one launch (start us, length us, event | category | flops | bytes accessed | tf_op | source)
XLA Modules:
  0.0 708.1 jit_solution(1049333634457209465)
XLA Ops:
  7.6 29.9 %all_gather.30 = bf16[3,70,1120]{1,0,2:T(4,128)(2,1)S(1)} all-gather(bf16[3,70,140]{1,0,2:T(4,128)(2,1)S(1)} %copy.37), channel_id=1, replica_groups=mesh['tm'=32,'space'=8] {'space'}, dimensions={2}, use_global_device_ids=true | all-gather | bytes 529200 | tf_op jit(solution)/shard_map/all_gather | solution.py:75
  37.4 1.4 copy.38
  38.8 5.7 stack.14
  44.6 7.6 %all-to-all-start = ((bf16[32,3,70,1120]{3,2,1,0:T(8,128)(2,1)}), bf16[32,3,70,1120]{3,2,1,0:T(8,128)(2,1)}, u32[]{:S(2)}, u32[]{:S(2)}) async-start(bf16[32,3,70,1120]{3,2,1,0:T(8,128)(2,1)} %stack.14), calls=%async_computation | async-start | bytes 31850496 | tf_op jit(solution)/shard_map/all_to_all | solution.py:80
  54.3 200.4 %all-to-all-done = bf16[32,3,70,1120]{3,2,1,0:T(8,128)(2,1)} async-done(((bf16[32,3,70,1120]{3,2,1,0:T(8,128)(2,1)}), bf16[32,3,70,1120]{3,2,1,0:T(8,128)(2,1)}, u32[]{:S(2)}, u32[]{:S(2)}) %all-to-all-start) | async-done | bytes 15052832 | tf_op jit(solution)/shard_map/all_to_all | solution.py:80
  254.8 13.5 %copy.39 = bf16[3,32,70,1120]{3,2,1,0:T(8,128)(2,1)} copy(bf16[3,32,70,1120]{3,2,0,1:T(8,128)(2,1)} %bitcast.9) | data formatting | bytes 30105600 | tf_op jit(solution)/shard_map/reshape | solution.py:79
  268.3 21.2 %reshape.69 = bf16[3,2240,1120]{2,1,0:T(8,128)(2,1)} reshape(bf16[3,32,70,1120]{3,2,1,0:T(8,128)(2,1)} %copy.39) | data formatting | bytes 30105600 | tf_op jit(solution)/shard_map/reshape | solution.py:79
  289.5 11.0 %convolution_bitcast_fusion = f32[3,448,1120]{2,1,0:T(8,128)S(1)} fusion(bf16[448,2240,1]{1,0,2:T(8,128)(2,1)S(1)} %bitcast.61, bf16[3,2240,1120]{2,1,0:T(8,128)(2,1)} %reshape.69), kind=kOutput, calls=%fused_computation.5 | convolution fusion | flops 6743654400 | bytes 23080960 | tf_op jit(solution)/shard_map/rn,cnh->crh/dot_general | solution.py:76
  300.5 2.6 copy-done
  304.3 3.4 reshape.95
  307.7 3.1 reshape.96
  310.9 3.1 fusion.11
  314.6 70.8 %all-reduce.6.cloned.1.call-done = f32[2,10,112,112]{3,2,1,0:T(8,128)} async-done(((f32[2,10,112,112]{3,2,1,0:T(8,128)}), f32[2,10,112,112]{3,2,1,0:T(8,128)}) %all-reduce.6.cloned.1.call-update) | async-done | bytes 1003536 | tf_op jit(solution)/shard_map/psum | solution.py:93
  385.4 4.7 fusion.15
  395.2 1.3 dynamic-update-slice.2
  397.2 63.4 %all-reduce.3 = (bf16[32]{0:T(256)(128)(2,1)S(1)}, bf16[32]{0:T(256)(128)(2,1)S(1)}, bf16[32]{0:T(256)(128)(2,1)S(1)}) all-reduce(bf16[32]{0:T(256)(128)(2,1)S(1)} %dynamic-update-slice, bf16[32]{0:T(256)(128)(2,1)S(1)} %dynamic-update-slice.1, bf16[32]{0:T(256)(128)(2,1)S(1)} %dynamic-update-slice.2), channel_id=1, replica_groups=mesh['tm'=32,'space'=8] {'tm'}, use_global_device_ids=true, to_apply=%add | all-reduce | flops 96 | bytes 384
  461.8 1.7 slice_maximum_fusion
  463.5 3.3 reshape.97
  466.8 185.5 %while.32 = (s32[]{:T(128)}, f32[]{:T(128)}, f32[]{:T(128)}, f32[10,112,112]{2,1,0:T(8,128)S(1)}, s32[]{:T(128)}, /*index=5*/bf16[32]{0:T(256)(128)(2,1)S(1)}, b...) while((s32[]{:T(128)}, f32[]{:T(128)}, f32[]{:T(128)}, ...), condition=%wide.region_7.8_spmd, body=%wide.region_6.7_spmd.sunk | while | flops 501773 | bytes 1254698 | solution.py:44
  652.5 38.9 %while.33 = (s32[]{:T(128)}, f32[10,112,112]{2,1,0:T(8,128)S(1)}, s32[]{:T(128)}, f32[32,10,112,112]{3,2,1,0:T(8,128)}, s32[]{:T(128)}, /*index=5*/s32[]{:T(128)}) while((s32[]{:T(128)}, f32[10,112,112]{2,1,0:T(8,128)S(1)}, s32[]{:T(128)}, f32[32,10,112,112]{3,2,1,0:T(8,128)}, s32[]{:T(128)}, /*index=5*/s32[]{:T(128)}) %tuple.71), condition=%wide.region_4.5_spmd.clone, body=%wide.region_3.4_spmd.clone.sunk | while | flops 376324 | bytes 1505373 | solution.py:19
  652.5 1.3 add_select_fusion.2
  691.4 3.3 fusion.10
  694.8 5.1 fusion.4
  700.2 1.4 copy.48
  (204 shorter events, 140.7 us)
Async XLA Ops:
  44.6 7.6 %copy-start.2 = (bf16[2,224,2240]{2,1,0:T(8,128)(2,1)S(1)}, bf16[2,224,2240]{2,1,0:T(8,128)(2,1)}, u32[]{:S(2)}) copy-start(bf16[2,224,2240]{2,1,0:T(8,128)(2,1)} %param.11) | copy-start | bytes 6021124
  44.6 8.1 %copy-start.6 = (f32[2240]{0:T(1024)S(1)}, f32[2240]{0:T(1024)}, u32[]{:S(2)}) copy-start(f32[2240]{0:T(1024)} %param.12) | copy-start | bytes 26884
  44.6 210.2 %all-to-all-start = ((bf16[32,3,70,1120]{3,2,1,0:T(8,128)(2,1)}), bf16[32,3,70,1120]{3,2,1,0:T(8,128)(2,1)}, u32[]{:S(2)}, u32[]{:S(2)}) async-start(bf16[32,3,70,1120]{3,2,1,0:T(8,128)(2,1)} %stack.14), calls=%async_computation | async-start | bytes 31850496 | tf_op jit(solution)/shard_map/all_to_all | solution.py:80
  52.1 333.3 %all-reduce.6.cloned.1.call-start = ((), (), s32[]{:S(2)}) async-start(), calls=%async_computation.1 | async-start | bytes 2293760 | tf_op jit(solution)/shard_map/psum | solution.py:93
  52.2 1.6 copy-start.3
  300.5 2.6 copy-start
  310.8 3.2 copy-start.8
  314.0 152.8 %all-gather.7.cloned.1.call-start = ((), (), s32[]{:S(2)}) async-start(), calls=%async_computation.3 | async-start | bytes 9461760 | tf_op jit(solution)/shard_map/all_gather | solution.py:27
  385.4 5.6 copy-start.4
  390.2 2.5 copy-start.9
  390.2 71.0 %copy-start.7 = (f32[1120]{0:T(1024)S(1)}, f32[1120]{0:T(1024)}, u32[]{:S(2)}) copy-start(f32[1120]{0:T(1024)} %param.16) | copy-start | bytes 13444
  391.0 261.5 %all-gather.5.cloned.1.call-start = ((), (), s32[]{:S(2)}) async-start(), calls=%async_computation.2 | async-start | bytes 18923520 | tf_op jit(solution)/shard_map/all_gather | solution.py:12
  652.5 38.9 %copy-start.5 = (f32[2,10,112,112]{3,2,1,0:T(8,128)S(1)}, f32[2,10,112,112]{3,2,1,0:T(8,128)}, u32[]{:S(2)}) copy-start(f32[2,10,112,112]{3,2,1,0:T(8,128)} %all-reduce.6.cloned.1.call-done) | copy-start | bytes 3010564
  691.4 3.3 copy-start.1
Sparse Core Ops, SparseCore 0:
  314.1 71.2 all-reduce.5
  391.1 58.7 all-gather.6
  452.5 80.7 all-gather.4
